TPU v7x, 128 devices: a whole 4x4x4 slice. The times are simulated.
128 devices in a mesh: ao: 32 (over x, y, z_hi), aux: 4 (over z_lo, core).
Axes of the slice: x: 4, y: 4, z: 4 (z_hi: 2, z_lo: 2; z = z_hi * 2 + z_lo), core: 2. Of those that a mesh axis runs over, the one named last changes fastest.
Arguments:
- tensor: bfloat16 [64, 4096, 384], P('aux', 'ao'), may hold values from -0.15625 to 0.15625
- pattern: int32 [64, 96], P('aux', 'ao'), may hold values 0 or 1
- occ_density: bfloat16 [4096, 384], P('ao'), may hold values from -0.3125 to 0.3125
- virt_density: bfloat16 [4096, 384], P('ao'), may hold values from -0.3125 to 0.3125
Outputs:
- polarizability: float32 [64, 64], P('aux')
All inputs are finite; a program needn't handle non-finite values. No bound on the sum of `pattern` on one device may be relied on, other than what follows from the above.
Results may differ from a plain program's by a relative error of at most 0.0041.
Values may be sent and summed in bfloat16 or wider, within the bound.
A program may use at most 128 MiB of HBM per device.

v0:
```python
import jax
import jax.numpy as jnp
from jax import lax
from jax.sharding import PartitionSpec as P

AB = 128


def extended(cells, sides, width):
    for axis, dim in sides:
        count = lax.axis_size(axis)
        head = lax.slice_in_dim(cells, 0, width, axis=dim)
        tail = lax.slice_in_dim(cells, cells.shape[dim] - width, cells.shape[dim], axis=dim)
        cells = jnp.concatenate(
            [
                lax.ppermute(tail, axis, [(i, (i + 1) % count) for i in range(count)]),
                cells,
                lax.ppermute(head, axis, [((i + 1) % count, i) for i in range(count)]),
            ],
            axis=dim,
        )
    return cells


def copy_for_each(shard, axis):
    size = lax.axis_size(axis)
    return lax.all_to_all(
        jnp.broadcast_to(shard[None], (size, *shard.shape)), axis, 0, 0, tiled=True
    )


def taken_together(shard, axis):
    everything = copy_for_each(shard, axis)
    return jnp.sum(everything, axis=0)


def occ_side(masked, occ_rims, blocks):
    aux_count = masked.shape[0]
    factor_rows = masked.reshape(aux_count, blocks, AB, 3, AB)
    partner = occ_rims.reshape(blocks + 2, AB, 3, AB)
    pieces = [None] * 5
    for offset_a in range(3):
        for offset_b in range(3):
            term = jnp.einsum(
                "qlik,lkj->qlij",
                factor_rows[:, :, :, offset_a, :],
                partner[offset_a : offset_a + blocks, :, offset_b, :],
                preferred_element_type=jnp.float32,
            )
            slot = offset_a + offset_b
            pieces[slot] = term if pieces[slot] is None else pieces[slot] + term
    return jnp.stack(pieces, axis=3).astype(jnp.bfloat16).reshape(aux_count, -1)


def virt_side(virt_density, tensor_rims, blocks):
    aux_count = tensor_rims.shape[0]
    factor_rows = virt_density.reshape(blocks, AB, 3, AB)
    partner = tensor_rims.reshape(aux_count, blocks + 2, AB, 3, AB)
    pieces = [None] * 5
    for offset_a in range(3):
        for offset_b in range(3):
            term = jnp.einsum(
                "lik,qlkj->qlij",
                factor_rows[:, :, offset_a, :],
                partner[:, offset_a : offset_a + blocks, :, offset_b, :],
                preferred_element_type=jnp.float32,
            )
            slot = offset_a + offset_b
            pieces[slot] = term if pieces[slot] is None else pieces[slot] + term
    return jnp.stack(pieces, axis=3).astype(jnp.bfloat16).reshape(aux_count, -1)


def on_device(tensor, pattern, occ_density, virt_density):
    aux_count = tensor.shape[0]
    blocks = tensor.shape[1] // AB
    masked = (
        tensor.reshape(aux_count, blocks, AB, 3, AB)
        * pattern.reshape(aux_count, blocks, 1, 3, 1).astype(jnp.bfloat16)
    ).reshape(tensor.shape)
    occ_rims = extended(occ_density, (("ao", 0),), AB)
    occ_flat = occ_side(masked, occ_rims, blocks)
    own_rims = extended(masked, (("ao", 1),), AB)
    virt_flat = virt_side(virt_density, own_rims, blocks)
    columns = jnp.einsum(
        "pl,ql->pq",
        occ_flat,
        lax.all_gather(virt_flat, "aux", axis=0, tiled=True),
        preferred_element_type=jnp.float32,
    )
    return taken_together(columns, "ao")


def solution(mesh):
    return jax.shard_map(
        on_device,
        mesh=mesh,
        in_specs=(P("aux", "ao", None), P("aux", "ao"), P("ao", None), P("ao", None)),
        out_specs=P("aux", None),
        check_vma=False,
    )
```

profile of v0, /device:TPU:1, one launch (start us, length us, event | category | flops | bytes accessed | tf_op | source)
XLA Modules:
  0.0 298.7 jit_solution(1570233315929819093)
XLA Ops:
  7.5 1.6 broadcast_multiply_fusion
  9.0 9.1 %collective-permute-start.3 = (bf16[16,128,384]{2,1,0:T(8,128)(2,1)S(1)}, bf16[16,128,384]{2,1,0:T(8,128)(2,1)S(1)}, u32[]{:S(2)}, u32[]{:S(2)}) collective-permute-start(bf16[16,128,384]{2,1,0:T(8,128)(2,1)S(1)} %broadcast_multiply_fusion), channel_id=1, source_target_pairs={{4,0},{8,4},{12,8},{16,12},{20,16},{24,20},{28,24},{32,28},{36,32}... | collective-permute-start | bytes 4718600 | tf_op jit(solution)/shard_map/ppermute | solution.py:18
  18.3 63.0 %collective-permute-done.3 = bf16[16,128,384]{2,1,0:T(8,128)(2,1)S(1)} collective-permute-done((bf16[16,128,384]{2,1,0:T(8,128)(2,1)S(1)}, bf16[16,128,384]{2,1,0:T(8,128)(2,1)S(1)}, u32[]{:S(2)}, u32[]{:S(2)}) %collective-permute-start.3) | collective-permute-done | bytes 1572896 | tf_op jit(solution)/shard_map/ppermute | solution.py:18
  82.2 3.6 %pad_maximum_fusion = bf16[16,384,384]{2,1,0:T(8,128)(2,1)} fusion(bf16[16,128,384]{2,1,0:T(8,128)(2,1)S(1)} %collective-permute-done.3, bf16[16,128,384]{2,1,0:T(8,128)(2,1)S(1)} %broadcast_multiply_fusion, bf16[16,128,384]{2,1,0:T(8,128)(2,1)} %collective-permute-done.2), kind=kLoop, calls=%fused_computation | loop fusion | flops 14155776 | bytes 9437184 | tf_op jit(solution)/shard_map/concatenate | solution.py:14
  85.9 12.9 %reshape.260 = bf16[16,3,128,3,128]{4,3,2,1,0:T(4,128)(2,1)} reshape(bf16[16,384,384]{2,1,0:T(8,128)(2,1)} %pad_maximum_fusion) | data formatting | bytes 9437184 | tf_op jit(solution)/shard_map/reshape | solution.py:58
  98.8 14.0 %fusion.50 = (bf16[16,1,128,1,128]{4,3,2,1,0:T(2,128)(2,1)S(1)}, bf16[16,1,128,1,128]{4,3,2,1,0:T(2,128)(2,1)S(1)}, bf16[16,1,128,1,128]{4,3,2,1,0:T(2,128)(2,1)...) fusion(bf16[16,3,128,3,128]{4,3,2,1,0:T(4,128)(2,1)} %reshape.260), kind=kLoop, calls=%fused_computation.73 | loop fusion | bytes 9437184 | tf_op jit(solution)/shard_map/slice | solution.py:65
  112.9 3.5 %copy.69 = bf16[16,1,128,1,128]{2,4,0,3,1:T(8,128)(2,1)} copy(bf16[16,1,128,1,128]{4,3,2,1,0:T(2,128)(2,1)} %get-tuple-element.13) | data formatting | bytes 1048576
  116.3 3.5 %copy.71 = bf16[16,1,128,1,128]{2,4,0,3,1:T(8,128)(2,1)} copy(bf16[16,1,128,1,128]{4,3,2,1,0:T(2,128)(2,1)} %get-tuple-element.12) | data formatting | bytes 1048576
  119.8 2.1 fusion.11
  121.9 2.3 fusion.35
  124.2 3.5 %copy.72 = bf16[16,1,128,1,128]{2,4,0,3,1:T(8,128)(2,1)} copy(bf16[16,1,128,1,128]{4,3,2,1,0:T(2,128)(2,1)} %get-tuple-element.11) | data formatting | bytes 1048576
  127.7 3.5 %copy.74 = bf16[16,1,128,1,128]{2,4,0,3,1:T(8,128)(2,1)} copy(bf16[16,1,128,1,128]{4,3,2,1,0:T(2,128)(2,1)} %get-tuple-element.10) | data formatting | bytes 1048576
  131.1 2.3 fusion.32
  133.4 3.5 %copy.75 = bf16[16,1,128,1,128]{2,4,0,3,1:T(8,128)(2,1)} copy(bf16[16,1,128,1,128]{4,3,2,1,0:T(2,128)(2,1)} %get-tuple-element.9) | data formatting | bytes 1048576
  136.9 3.5 %copy.76 = bf16[16,1,128,1,128]{2,4,0,3,1:T(8,128)(2,1)} copy(bf16[16,1,128,1,128]{4,3,2,1,0:T(2,128)(2,1)} %get-tuple-element.8) | data formatting | bytes 1048576
  140.4 1.8 copy.78
  142.2 2.3 fusion.28
  144.5 1.8 copy.79
  147.0 1.7 convolution_add_fusion.2
  153.1 6.1 %copy.59 = bf16[16,1,128,5,128]{4,3,2,0,1:T(8,128)(2,1)} copy(bf16[16,1,128,5,128]{2,4,0,3,1:T(8,128)(2,1)} %fusion.13) | data formatting | bytes 5242880 | tf_op jit(solution)/shard_map/stack | solution.py:70
  159.2 5.5 %convert_element_type.20 = bf16[16,81920]{1,0:T(8,128)(2,1)} reshape(bf16[16,1,128,5,128]{4,3,2,0,1:T(8,128)(2,1)} %copy.59) | data formatting | bytes 5242880 | tf_op jit(solution)/shard_map/convert_element_type | solution.py:70
  165.6 6.7 %collective-permute-start.1 = (bf16[128,384]{1,0:T(8,128)(2,1)S(1)}, bf16[128,384]{1,0:T(8,128)(2,1)S(1)}, u32[]{:S(2)}, u32[]{:S(2)}) collective-permute-start(bf16[128,384]{1,0:T(8,128)(2,1)S(1)} %copy-done.6), channel_id=1, source_target_pairs={{4,0},{8,4},{12,8},{16,12},{20,16},{24,20},{28,24},{32,28},{36,32}... | collective-permute-start | bytes 294920 | tf_op jit(solution)/shard_map/ppermute | solution.py:18
  172.3 1.6 copy.34
  173.9 1.9 copy.35
  176.0 5.5 %collective-permute-done = bf16[128,384]{1,0:T(8,128)(2,1)S(1)} collective-permute-done((bf16[128,384]{1,0:T(8,128)(2,1)S(1)}, bf16[128,384]{1,0:T(8,128)(2,1)S(1)}, u32[]{:S(2)}, u32[]{:S(2)}) %collective-permute-start) | collective-permute-done | bytes 98336 | tf_op jit(solution)/shard_map/ppermute | solution.py:16
  185.2 1.1 fusion.25
  188.8 1.1 fusion.9
  189.9 6.1 %copy.44 = bf16[16,1,128,5,128]{4,3,2,0,1:T(8,128)(2,1)} copy(bf16[16,1,128,5,128]{2,4,0,3,1:T(8,128)(2,1)} %fusion.9) | data formatting | bytes 5242880 | tf_op jit(solution)/shard_map/stack | solution.py:52
  196.1 4.5 %convert_element_type.19 = bf16[16,81920]{1,0:T(8,128)(2,1)S(1)} reshape(bf16[16,1,128,5,128]{4,3,2,0,1:T(8,128)(2,1)} %copy.44) | data formatting | bytes 5242880 | tf_op jit(solution)/shard_map/convert_element_type | solution.py:52
  200.5 65.5 %all-gather.2.cloned.1.call-done = bf16[64,81920]{1,0:T(8,128)(2,1)} async-done(((bf16[16,81920]{1,0:T(8,128)(2,1)}), bf16[64,81920]{1,0:T(8,128)(2,1)}) %all-gather.2.cloned.1.call-update) | async-done | bytes 10485776 | tf_op jit(solution)/shard_map/all_gather | solution.py:87
  266.0 5.5 %fusion.52 = f32[16,64]{1,0:T(8,128)S(1)} fusion(bf16[16,81920]{1,0:T(8,128)(2,1)S(1)} %convert_element_type.19, bf16[64,81920]{1,0:T(8,128)(2,1)} %all-gather.2.cloned.1.call-done), kind=kOutput, calls=%fused_computation.75 | convolution fusion | flops 167772160 | bytes 13111296 | tf_op jit(solution)/shard_map/pl,ql->pq/dot_general | solution.py:84
  271.7 17.9 %all_to_all.5 = f32[32,1,1024]{2,1,0:T(1,128)S(1)} all-to-all(f32[32,1,1024]{2,1,0:T(1,128)S(1)} %reshape.286), channel_id=1, replica_groups=mesh['ao'=32,'aux'=4] {'ao'}, dimensions={0} | all-to-all | bytes 262144 | tf_op jit(solution)/shard_map/all_to_all | solution.py:27
  (58 shorter events, 16.7 us)
Async XLA Ops:
  6.5 11.6 %copy-start.7 = (bf16[128,384]{1,0:T(8,128)(2,1)S(1)}, bf16[128,384]{1,0:T(8,128)(2,1)}, u32[]{:S(2)}) copy-start(bf16[128,384]{1,0:T(8,128)(2,1)} %param.7) | copy-start | bytes 294916
  6.5 259.5 %all-gather.2.cloned.1.call-start = ((), (), s32[]{:S(2)}) async-start(), calls=%async_computation.1 | async-start | bytes 13107200 | tf_op jit(solution)/shard_map/all_gather | solution.py:87
  9.0 72.3 %collective-permute-start.3 = (bf16[16,128,384]{2,1,0:T(8,128)(2,1)S(1)}, bf16[16,128,384]{2,1,0:T(8,128)(2,1)S(1)}, u32[]{:S(2)}, u32[]{:S(2)}) collective-permute-start(bf16[16,128,384]{2,1,0:T(8,128)(2,1)S(1)} %broadcast_multiply_fusion), channel_id=1, source_target_pairs={{4,0},{8,4},{12,8},{16,12},{20,16},{24,20},{28,24},{32,28},{36,32}... | collective-permute-start | bytes 4718600 | tf_op jit(solution)/shard_map/ppermute | solution.py:18
  18.2 64.1 %collective-permute-start.2 = (bf16[16,128,384]{2,1,0:T(8,128)(2,1)S(1)}, bf16[16,128,384]{2,1,0:T(8,128)(2,1)}, u32[]{:S(2)}, u32[]{:S(2)}) collective-permute-start(bf16[16,128,384]{2,1,0:T(8,128)(2,1)S(1)} %broadcast_multiply_fusion), channel_id=1, source_target_pairs={{0,4},{4,8},{8,12},{12,16},{16,20},{20,24},{24,28},{28,32},{32,36}... | collective-permute-start | bytes 4718600 | tf_op jit(solution)/shard_map/ppermute | solution.py:16
  144.5 4.2 %copy-start.1 = (f32[16,128,128]{2,1,0:T(8,128)S(1)}, f32[16,128,128]{2,1,0:T(8,128)}, u32[]{:S(2)}) copy-start(f32[16,128,128]{2,1,0:T(8,128)} %fusion.35) | copy-start | bytes 3145732
  146.3 2.5 copy-start.3
  147.0 2.9 copy-start.4
  148.8 2.2 copy-start.2
  148.8 2.2 copy-start.5
  164.7 0.9 copy-start.6
  164.7 7.6 %copy-start = (bf16[16,128,384]{2,1,0:T(8,128)(2,1)S(1)}, bf16[16,128,384]{2,1,0:T(8,128)(2,1)}, u32[]{:S(2)}) copy-start(bf16[16,128,384]{2,1,0:T(8,128)(2,1)} %param.4) | copy-start | bytes 4718596
  165.6 10.4 %collective-permute-start.1 = (bf16[128,384]{1,0:T(8,128)(2,1)S(1)}, bf16[128,384]{1,0:T(8,128)(2,1)S(1)}, u32[]{:S(2)}, u32[]{:S(2)}) collective-permute-start(bf16[128,384]{1,0:T(8,128)(2,1)S(1)} %copy-done.6), channel_id=1, source_target_pairs={{4,0},{8,4},{12,8},{16,12},{20,16},{24,20},{28,24},{32,28},{36,32}... | collective-permute-start | bytes 294920 | tf_op jit(solution)/shard_map/ppermute | solution.py:18
  172.3 9.2 %collective-permute-start = (bf16[128,384]{1,0:T(8,128)(2,1)S(1)}, bf16[128,384]{1,0:T(8,128)(2,1)S(1)}, u32[]{:S(2)}, u32[]{:S(2)}) collective-permute-start(bf16[128,384]{1,0:T(8,128)(2,1)S(1)} %copy-done.6), channel_id=1, source_target_pairs={{0,4},{4,8},{8,12},{12,16},{16,20},{20,24},{24,28},{28,32},{32,36}... | collective-permute-start | bytes 294920 | tf_op jit(solution)/shard_map/ppermute | solution.py:16
Sparse Core Ops, SparseCore 0:
  164.8 101.1 all-gather.1
where the time goes:
time: 300 us; the launch traced here: 299 us
  waiting for transfers between devices  135 us (45%)
  local copies, waits for them, and re-layouts  81.4 us (27%)
  matrix products  27.3 us (9%)
  blocking collectives  17.9 us (6%)
  starting transfers between devices  15.8 us (5%)
  between operations  13.6 us (5%)
  other arithmetic  7.71 us (3%)
    all_gather x1, waiting for transfers between devices, on_device(): lax.all_gather(virt_flat, 'aux', axis=0, tiled=True)  65.5 us
    ppermute x2, waiting for transfers between devices, extended(): lax.ppermute(head, axis, [((i + 1) % count, i) for i in range(count)])  63.1 us
    unnamed x39, local copies, waits for them, and re-layouts  29.1 us
    all_to_all x1, blocking collectives, copy_for_each(): lax.all_to_all(jnp.broadcast_to(shard[None], (size, *shard.shape)), axis,...  17.9 us
    ppermute x2, starting transfers between devices, extended(): lax.ppermute(head, axis, [((i + 1) % count, i) for i in range(count)])  15.8 us
    dot_general x9, matrix products, virt_side(): jnp.einsum('lik,qlkj->qlij', factor_rows[:, :, offset_a, :], partner[:, o...  15.1 us
    slice x1, local copies, waits for them, and re-layouts, virt_side(): partner[:, offset_a:offset_a + blocks, :, offset_b, :]  14 us
    reshape x1, local copies, waits for them, and re-layouts, virt_side(): partner = tensor_rims.reshape(aux_count, blocks + 2, AB, 3, AB)  12.9 us
  transfers between devices with their start and end apart: 5, of which 4 were waited for; matrix products, arithmetic and copies ran while one was open for 8% of the time, Pallas kernels for 0%

commit v1 on v0

--- a/solution.py
+++ b/solution.py
@@ -4,6 +4,11 @@
 from jax.sharding import PartitionSpec as P
 
 AB = 128
+
+
+def exchange_gather(array, mesh_axis, dim):
+    sent = jnp.stack([array] * lax.axis_size(mesh_axis))
+    return jnp.concatenate(lax.all_to_all(sent, mesh_axis, 0, 0), axis=dim)
 
 
 def extended(cells, sides, width):
@@ -84,7 +89,7 @@
     columns = jnp.einsum(
         "pl,ql->pq",
         occ_flat,
-        lax.all_gather(virt_flat, "aux", axis=0, tiled=True),
+        exchange_gather(virt_flat, "aux", 0),
         preferred_element_type=jnp.float32,
     )
     return taken_together(columns, "ao")

time: 300 us -> 334 us (1.11)
  waiting for transfers between devices: 135 us -> 172 us
  between operations: 13.6 us -> 0.26 us
  starting transfers between devices: 15.8 us -> 24.4 us
    ppermute x2, waiting for transfers between devices: 6.36 us -> 168 us  [extended(): lax.ppermute(tail, axis, [(i, (i + 1) % count) for i in range(count)])]
    all_gather x1 -> x0, waiting for transfers between devices: 65.5 us -> none  [on_device(): lax.all_gather(virt_flat, 'aux', axis=0, tiled=True)]
    ppermute x2, waiting for transfers between devices: 63.1 us -> 4.07 us  [extended(): lax.ppermute(head, axis, [((i + 1) % count, i) for i in range(count)])]
    all_to_all x0 -> x1, starting transfers between devices: none -> 8 us  [exchange_gather(): return jnp.concatenate(lax.all_to_all(sent, mesh_axis, 0, 0), axis=dim)]
    another operation x0 -> x1, local copies, waits for them, and re-layouts: none -> 4.5 us  [exchange_gather(): sent = jnp.stack([array] * lax.axis_size(mesh_axis))]
    ppermute x2, starting transfers between devices: 0.01 us -> 4.5 us  [extended(): lax.ppermute(tail, axis, [(i, (i + 1) % count) for i in range(count)])]
    ppermute x2, starting transfers between devices: 15.8 us -> 11.9 us  [extended(): lax.ppermute(head, axis, [((i + 1) % count, i) for i in range(count)])]
  transfers between devices with their start and end apart: 5 -> 5, of which waited for: 4 -> 4; matrix products, arithmetic and copies ran while one was open for 8% -> 7% of each run, Pallas kernels for 0% -> 0%
where the time goes in v1:
time: 334 us; the launch traced here: 332 us
  waiting for transfers between devices  172 us (51%)
  local copies, waits for them, and re-layouts  84.3 us (25%)
  matrix products  27.5 us (8%)
  starting transfers between devices  24.4 us (7%)
  blocking collectives  15.8 us (5%)
  other arithmetic  7.7 us (2%)
    ppermute x2, waiting for transfers between devices, extended(): lax.ppermute(tail, axis, [(i, (i + 1) % count) for i in range(count)])  168 us
    unnamed x39, local copies, waits for them, and re-layouts  28.4 us
    all_to_all x1, blocking collectives, copy_for_each(): lax.all_to_all(jnp.broadcast_to(shard[None], (size, *shard.shape)), axis,...  15.8 us
    dot_general x9, matrix products, virt_side(): jnp.einsum('lik,qlkj->qlij', factor_rows[:, :, offset_a, :], partner[:, o...  15.1 us
    slice x1, local copies, waits for them, and re-layouts, virt_side(): partner[:, offset_a:offset_a + blocks, :, offset_b, :]  14.1 us
    reshape x1, local copies, waits for them, and re-layouts, virt_side(): partner = tensor_rims.reshape(aux_count, blocks + 2, AB, 3, AB)  12.9 us
    ppermute x2, starting transfers between devices, extended(): lax.ppermute(head, axis, [((i + 1) % count, i) for i in range(count)])  11.9 us
    all_to_all x1, starting transfers between devices, exchange_gather(): return jnp.concatenate(lax.all_to_all(sent, mesh_axis, 0, 0), axis=dim)  8 us
  transfers between devices with their start and end apart: 5, of which 4 were waited for; matrix products, arithmetic and copies ran while one was open for 7% of the time, Pallas kernels for 0%

profile of v1, /device:TPU:1, one launch (start us, length us, event | category | flops | bytes accessed | tf_op | source)
XLA Modules:
  0.0 332.1 jit_solution(645961900090640807)
XLA Ops:
  2.5 4.5 %collective-permute-start.2 = (bf16[16,128,384]{2,1,0:T(8,128)(2,1)S(1)}, bf16[16,128,384]{2,1,0:T(8,128)(2,1)S(1)}, u32[]{:S(2)}, u32[]{:S(2)}) collective-permute-start(bf16[16,128,384]{2,1,0:T(8,128)(2,1)S(1)} %broadcast_multiply_fusion), channel_id=1, source_target_pairs={{0,4},{4,8},{8,12},{12,16},{16,20},{20,24},{24,28},{28,32},{32,36}... | collective-permute-start | bytes 4718600 | tf_op jit(solution)/shard_map/ppermute | solution.py:21
  7.0 4.7 %collective-permute-start.3 = (bf16[16,128,384]{2,1,0:T(8,128)(2,1)S(1)}, bf16[16,128,384]{2,1,0:T(8,128)(2,1)}, u32[]{:S(2)}, u32[]{:S(2)}) collective-permute-start(bf16[16,128,384]{2,1,0:T(8,128)(2,1)S(1)} %broadcast_multiply_fusion), channel_id=1, source_target_pairs={{4,0},{8,4},{12,8},{16,12},{20,16},{24,20},{28,24},{32,28},{36,32}... | collective-permute-start | bytes 4718600 | tf_op jit(solution)/shard_map/ppermute | solution.py:23
  11.8 61.9 %collective-permute-done.2 = bf16[16,128,384]{2,1,0:T(8,128)(2,1)S(1)} collective-permute-done((bf16[16,128,384]{2,1,0:T(8,128)(2,1)S(1)}, bf16[16,128,384]{2,1,0:T(8,128)(2,1)S(1)}, u32[]{:S(2)}, u32[]{:S(2)}) %collective-permute-start.2) | collective-permute-done | bytes 1572896 | tf_op jit(solution)/shard_map/ppermute | solution.py:21
  73.8 3.5 %collective-permute-done.3 = bf16[16,128,384]{2,1,0:T(8,128)(2,1)} collective-permute-done((bf16[16,128,384]{2,1,0:T(8,128)(2,1)S(1)}, bf16[16,128,384]{2,1,0:T(8,128)(2,1)}, u32[]{:S(2)}, u32[]{:S(2)}) %collective-permute-start.3) | collective-permute-done | bytes 1572896 | tf_op jit(solution)/shard_map/ppermute | solution.py:23
  77.2 3.6 %pad_maximum_fusion = bf16[16,384,384]{2,1,0:T(8,128)(2,1)} fusion(bf16[16,128,384]{2,1,0:T(8,128)(2,1)} %collective-permute-done.3, bf16[16,128,384]{2,1,0:T(8,128)(2,1)S(1)} %broadcast_multiply_fusion, bf16[16,128,384]{2,1,0:T(8,128)(2,1)S(1)} %collective-permute-done.2), kind=kLoop, calls=%fused_computation | loop fusion | flops 14155776 | bytes 9437184 | tf_op jit(solution)/shard_map/concatenate | solution.py:19
  80.9 12.9 %reshape.333 = bf16[16,3,128,3,128]{4,3,2,1,0:T(4,128)(2,1)} reshape(bf16[16,384,384]{2,1,0:T(8,128)(2,1)} %pad_maximum_fusion) | data formatting | bytes 9437184 | tf_op jit(solution)/shard_map/reshape | solution.py:63
  93.8 14.1 %fusion.50 = (bf16[16,1,128,1,128]{4,3,2,1,0:T(2,128)(2,1)S(1)}, bf16[16,1,128,1,128]{4,3,2,1,0:T(2,128)(2,1)S(1)}, bf16[16,1,128,1,128]{4,3,2,1,0:T(2,128)(2,1)...) fusion(bf16[16,3,128,3,128]{4,3,2,1,0:T(4,128)(2,1)} %reshape.333), kind=kLoop, calls=%fused_computation.73 | loop fusion | bytes 9437184 | tf_op jit(solution)/shard_map/slice | solution.py:70
  108.0 3.5 %copy.69 = bf16[16,1,128,1,128]{2,4,0,3,1:T(8,128)(2,1)} copy(bf16[16,1,128,1,128]{4,3,2,1,0:T(2,128)(2,1)} %get-tuple-element.13) | data formatting | bytes 1048576
  111.4 3.5 %copy.71 = bf16[16,1,128,1,128]{2,4,0,3,1:T(8,128)(2,1)} copy(bf16[16,1,128,1,128]{4,3,2,1,0:T(2,128)(2,1)} %get-tuple-element.12) | data formatting | bytes 1048576
  114.9 2.1 fusion.11
  117.1 2.3 fusion.35
  119.4 3.5 %copy.72 = bf16[16,1,128,1,128]{2,4,0,3,1:T(8,128)(2,1)} copy(bf16[16,1,128,1,128]{4,3,2,1,0:T(2,128)(2,1)} %get-tuple-element.11) | data formatting | bytes 1048576
  122.8 3.5 %copy.74 = bf16[16,1,128,1,128]{2,4,0,3,1:T(8,128)(2,1)} copy(bf16[16,1,128,1,128]{4,3,2,1,0:T(2,128)(2,1)} %get-tuple-element.10) | data formatting | bytes 1048576
  126.3 2.3 fusion.32
  128.6 3.5 %copy.75 = bf16[16,1,128,1,128]{2,4,0,3,1:T(8,128)(2,1)} copy(bf16[16,1,128,1,128]{4,3,2,1,0:T(2,128)(2,1)} %get-tuple-element.9) | data formatting | bytes 1048576
  132.1 3.5 %copy.76 = bf16[16,1,128,1,128]{2,4,0,3,1:T(8,128)(2,1)} copy(bf16[16,1,128,1,128]{4,3,2,1,0:T(2,128)(2,1)} %get-tuple-element.8) | data formatting | bytes 1048576
  135.6 1.8 copy.78
  137.4 2.3 fusion.28
  139.7 1.8 copy.79
  142.3 1.7 convolution_add_fusion.2
  148.4 6.1 %copy.59 = bf16[16,1,128,5,128]{4,3,2,0,1:T(8,128)(2,1)} copy(bf16[16,1,128,5,128]{2,4,0,3,1:T(8,128)(2,1)} %fusion.13) | data formatting | bytes 5242880 | tf_op jit(solution)/shard_map/stack | solution.py:75
  154.4 4.5 %convert_element_type.33 = bf16[16,81920]{1,0:T(8,128)(2,1)S(1)} reshape(bf16[16,1,128,5,128]{4,3,2,0,1:T(8,128)(2,1)} %copy.59) | data formatting | bytes 5242880 | tf_op jit(solution)/shard_map/convert_element_type | solution.py:75
  158.9 4.5 %stack.51 = bf16[4,16,81920]{2,1,0:T(8,128)(2,1)} broadcast(bf16[16,81920]{1,0:T(8,128)(2,1)S(1)} %convert_element_type.33), dimensions={1,2} | broadcast | bytes 13107200 | tf_op jit(solution)/shard_map/stack | solution.py:10
  163.4 8.0 %all-to-all-start = ((bf16[4,16,81920]{2,1,0:T(8,128)(2,1)}), bf16[4,16,81920]{2,1,0:T(8,128)(2,1)}, u32[]{:S(2)}, u32[]{:S(2)}) async-start(bf16[4,16,81920]{2,1,0:T(8,128)(2,1)} %stack.51), calls=%async_computation | async-start | bytes 20971520 | tf_op jit(solution)/shard_map/all_to_all | solution.py:11
  171.4 7.2 %collective-permute-start.1 = (bf16[128,384]{1,0:T(8,128)(2,1)S(1)}, bf16[128,384]{1,0:T(8,128)(2,1)S(1)}, u32[]{:S(2)}, u32[]{:S(2)}) collective-permute-start(bf16[128,384]{1,0:T(8,128)(2,1)S(1)} %copy-done.6), channel_id=1, source_target_pairs={{4,0},{8,4},{12,8},{16,12},{20,16},{24,20},{28,24},{32,28},{36,32}... | collective-permute-start | bytes 294920 | tf_op jit(solution)/shard_map/ppermute | solution.py:23
  178.6 1.6 copy.34
  180.2 1.9 copy.35
  182.3 106.1 %collective-permute-done = bf16[128,384]{1,0:T(8,128)(2,1)S(1)} collective-permute-done((bf16[128,384]{1,0:T(8,128)(2,1)S(1)}, bf16[128,384]{1,0:T(8,128)(2,1)S(1)}, u32[]{:S(2)}, u32[]{:S(2)}) %collective-permute-start) | collective-permute-done | bytes 98336 | tf_op jit(solution)/shard_map/ppermute | solution.py:21
  297.7 6.1 %copy.44 = bf16[16,1,128,5,128]{4,3,2,0,1:T(8,128)(2,1)} copy(bf16[16,1,128,5,128]{2,4,0,3,1:T(8,128)(2,1)} %fusion.9) | data formatting | bytes 5242880 | tf_op jit(solution)/shard_map/stack | solution.py:57
  303.8 4.5 %convert_element_type.32 = bf16[16,81920]{1,0:T(8,128)(2,1)S(1)} reshape(bf16[16,1,128,5,128]{4,3,2,0,1:T(8,128)(2,1)} %copy.44) | data formatting | bytes 5242880 | tf_op jit(solution)/shard_map/convert_element_type | solution.py:57
  308.3 5.5 %fusion.52 = f32[16,64]{1,0:T(8,128)S(1)} fusion(bf16[16,81920]{1,0:T(8,128)(2,1)S(1)} %convert_element_type.32, bf16[64,81920]{1,0:T(8,128)(2,1)} %bitcast.71), kind=kOutput, calls=%fused_computation.75 | convolution fusion | flops 167772160 | bytes 13111296 | tf_op jit(solution)/shard_map/pl,ql->pq/dot_general | solution.py:89
  314.0 15.8 %all_to_all.10 = f32[32,1,1024]{2,1,0:T(1,128)S(1)} all-to-all(f32[32,1,1024]{2,1,0:T(1,128)S(1)} %reshape.360), channel_id=1, replica_groups=mesh['ao'=32,'aux'=4] {'ao'}, dimensions={0} | all-to-all | bytes 262144 | tf_op jit(solution)/shard_map/all_to_all | solution.py:32
  (58 shorter events, 19.4 us)
Async XLA Ops:
  0.0 11.7 %copy-start.7 = (bf16[128,384]{1,0:T(8,128)(2,1)S(1)}, bf16[128,384]{1,0:T(8,128)(2,1)}, u32[]{:S(2)}) copy-start(bf16[128,384]{1,0:T(8,128)(2,1)} %param.7) | copy-start | bytes 294916
  2.5 71.3 %collective-permute-start.2 = (bf16[16,128,384]{2,1,0:T(8,128)(2,1)S(1)}, bf16[16,128,384]{2,1,0:T(8,128)(2,1)S(1)}, u32[]{:S(2)}, u32[]{:S(2)}) collective-permute-start(bf16[16,128,384]{2,1,0:T(8,128)(2,1)S(1)} %broadcast_multiply_fusion), channel_id=1, source_target_pairs={{0,4},{4,8},{8,12},{12,16},{16,20},{20,24},{24,28},{28,32},{32,36}... | collective-permute-start | bytes 4718600 | tf_op jit(solution)/shard_map/ppermute | solution.py:21
  7.0 70.3 %collective-permute-start.3 = (bf16[16,128,384]{2,1,0:T(8,128)(2,1)S(1)}, bf16[16,128,384]{2,1,0:T(8,128)(2,1)}, u32[]{:S(2)}, u32[]{:S(2)}) collective-permute-start(bf16[16,128,384]{2,1,0:T(8,128)(2,1)S(1)} %broadcast_multiply_fusion), channel_id=1, source_target_pairs={{4,0},{8,4},{12,8},{16,12},{20,16},{24,20},{28,24},{32,28},{36,32}... | collective-permute-start | bytes 4718600 | tf_op jit(solution)/shard_map/ppermute | solution.py:23
  139.7 4.2 %copy-start.1 = (f32[16,128,128]{2,1,0:T(8,128)S(1)}, f32[16,128,128]{2,1,0:T(8,128)}, u32[]{:S(2)}) copy-start(f32[16,128,128]{2,1,0:T(8,128)} %fusion.35) | copy-start | bytes 3145732
  141.5 2.5 copy-start.3
  142.2 2.8 copy-start.4
  144.0 2.2 copy-start.2
  144.0 2.2 copy-start.5
  163.4 8.0 %copy-start.6 = (bf16[128,384]{1,0:T(8,128)(2,1)S(1)}, bf16[128,384]{1,0:T(8,128)(2,1)}, u32[]{:S(2)}) copy-start(bf16[128,384]{1,0:T(8,128)(2,1)} %param.6) | copy-start | bytes 294916
  163.4 15.2 %copy-start = (bf16[16,128,384]{2,1,0:T(8,128)(2,1)S(1)}, bf16[16,128,384]{2,1,0:T(8,128)(2,1)}, u32[]{:S(2)}) copy-start(bf16[16,128,384]{2,1,0:T(8,128)(2,1)} %param.4) | copy-start | bytes 4718596
  163.4 144.9 %all-to-all-start = ((bf16[4,16,81920]{2,1,0:T(8,128)(2,1)}), bf16[4,16,81920]{2,1,0:T(8,128)(2,1)}, u32[]{:S(2)}, u32[]{:S(2)}) async-start(bf16[4,16,81920]{2,1,0:T(8,128)(2,1)} %stack.51), calls=%async_computation | async-start | bytes 20971520 | tf_op jit(solution)/shard_map/all_to_all | solution.py:11
  171.4 117.1 %collective-permute-start = (bf16[128,384]{1,0:T(8,128)(2,1)S(1)}, bf16[128,384]{1,0:T(8,128)(2,1)S(1)}, u32[]{:S(2)}, u32[]{:S(2)}) collective-permute-start(bf16[128,384]{1,0:T(8,128)(2,1)S(1)} %copy-done.6), channel_id=1, source_target_pairs={{0,4},{4,8},{8,12},{12,16},{16,20},{20,24},{24,28},{28,32},{32,36}... | collective-permute-start | bytes 294920 | tf_op jit(solution)/shard_map/ppermute | solution.py:21
  171.4 117.6 %collective-permute-start.1 = (bf16[128,384]{1,0:T(8,128)(2,1)S(1)}, bf16[128,384]{1,0:T(8,128)(2,1)S(1)}, u32[]{:S(2)}, u32[]{:S(2)}) collective-permute-start(bf16[128,384]{1,0:T(8,128)(2,1)S(1)} %copy-done.6), channel_id=1, source_target_pairs={{4,0},{8,4},{12,8},{16,12},{20,16},{24,20},{28,24},{32,28},{36,32}... | collective-permute-start | bytes 294920 | tf_op jit(solution)/shard_map/ppermute | solution.py:23
